TPU v7x, 32 devices: a whole 2x2x4 slice. The times are simulated.
32 devices in a mesh: dp: 4 (over y, x), fsdp: 4 (over z), ctx: 2 (over core).
Axes of the slice: x: 2, y: 2, z: 4, core: 2. Of those that a mesh axis runs over, the one named last changes fastest.
Arguments:
- inputs: bfloat16 [16, 1024, 1024], P(('dp', 'fsdp'), 'ctx'), may hold values from -6 to 6
- lengths: int32 [16], P(('dp', 'fsdp')), may hold values from 256 to 1024, as said below
- cotangent: bfloat16 [16, 1024, 1024], P(('dp', 'fsdp'), 'ctx'), may hold values from -6 to 6
- norm_gain1: float32 [1024], replicated, may hold values from 0.5 to 1.5
- w_qkv: bfloat16 [1024, 3072], P('fsdp'), may hold values from -0.1875 to 0.1875
- w_beta: bfloat16 [1024, 8], P('fsdp'), may hold values from -0.1875 to 0.1875
- conv_weight: float32 [4, 3072], replicated, may hold values from -3 to 3
- head_gain: float32 [128], replicated, may hold values from 0.5 to 1.5
- w_out: bfloat16 [1024, 1024], P('fsdp'), may hold values from -0.1875 to 0.1875
- norm_gain2: float32 [1024], replicated, may hold values from 0.5 to 1.5
- w_gateup: bfloat16 [1024, 5632], P('fsdp'), may hold values from -0.1875 to 0.1875
- w_down: bfloat16 [2816, 1024], P('fsdp'), may hold values from -0.109375 to 0.109375
Outputs:
- output: bfloat16 [16, 1024, 1024], P(('dp', 'fsdp'), 'ctx')
- grad_inputs: bfloat16 [16, 1024, 1024], P(('dp', 'fsdp'), 'ctx')
- grad_gain1: float32 [1024], replicated
- grad_qkv: float32 [1024, 3072], P(('fsdp', 'ctx'))
- grad_beta: float32 [1024, 8], P(('fsdp', 'ctx'))
- grad_conv: float32 [4, 3072], replicated
- grad_head_gain: float32 [128], replicated
- grad_out: float32 [1024, 1024], P(('fsdp', 'ctx'))
- grad_gain2: float32 [1024], replicated
- grad_gateup: float32 [1024, 5632], P(('fsdp', 'ctx'))
- grad_down: float32 [2816, 1024], P(('fsdp', 'ctx'))
Inputs may be any that keep to these rules, and one draw needn't show every extreme that they name: `lengths`: valid tokens of each sequence; they come first in it. Some sequence has all 1024 positions valid and some sequence has 256.
All inputs are finite; a program needn't handle non-finite values.
Results may differ from a plain program's by a relative error of at most 0.014.
Values may be sent and summed in bfloat16 or wider, within the bound.
No kernel may reach another device: no remote copies, remote signals or barrier semaphores. Data moves between devices by JAX's collectives and lax.ppermute only.
A program may use at most 256 MiB of HBM per device.

v0:
```python
import jax
import jax.numpy as jnp
from jax import lax
from jax.sharding import PartitionSpec as P

H = 8
HD = 128
KERNEL = 4
SPAN = 64
exact_precision = lax.Precision.HIGHEST


def passed_along(value, axis, steps):
    count = lax.axis_size(axis)
    first, last = (max(0, -steps), min(count, count - steps))
    return lax.ppermute(value, axis, [(source, source + steps) for source in range(first, last)])


def as_sent(value):
    return jax.tree.map(lambda a: a.astype(jnp.bfloat16) if a.dtype == jnp.float32 else a, value)


def span_factors(key_row_block, value_rows, strength):
    block_len = key_row_block.shape[1]
    head_width = key_row_block.shape[2]
    gram_matrix = jnp.einsum(
        "hik,hjk->hij", key_row_block, key_row_block, precision=exact_precision
    )
    system = jnp.tril(gram_matrix * strength[:, :, None], -1) + jnp.eye(
        block_len, dtype=key_row_block.dtype
    )
    right_side = strength[:, :, None] * jnp.concatenate([key_row_block, value_rows], -1)
    solved = jax.scipy.linalg.solve_triangular(system, right_side, lower=True, unit_diagonal=True)
    return (solved[..., :head_width], solved[..., head_width:])


def span_output(memory_matrix, blocks):
    query_rows, key_row_block, value_rows, strength = blocks
    key_blend, value_blend = span_factors(key_row_block, value_rows, strength)
    prediction_error = value_blend - jnp.einsum(
        "ist,itn->isn", key_blend, memory_matrix, precision=exact_precision
    )
    scores = jnp.tril(
        jnp.einsum("hik,hjk->hij", query_rows, key_row_block, precision=exact_precision)
    )
    final_result = jnp.einsum("ist,itn->isn", query_rows, memory_matrix, precision=exact_precision)
    final_result = final_result + jnp.einsum(
        "hij,hjv->hiv", scores, prediction_error, precision=exact_precision
    )
    updated_memory = memory_matrix + jnp.einsum(
        "xzn,xzf->xnf", key_row_block, prediction_error, precision=exact_precision
    )
    return (updated_memory, final_result)


def span_advance(carry, blocks):
    memory_matrix, transition = carry
    key_row_block, value_rows, strength = blocks
    key_blend, value_blend = span_factors(key_row_block, value_rows, strength)
    prediction_error = value_blend - jnp.einsum(
        "ist,itn->isn", key_blend, memory_matrix, precision=exact_precision
    )
    memory_matrix = memory_matrix + jnp.einsum(
        "xzn,xzf->xnf", key_row_block, prediction_error, precision=exact_precision
    )
    identity = jnp.eye(key_row_block.shape[2], dtype=key_row_block.dtype)
    step_map = identity - jnp.einsum(
        "hck,hcl->hkl", key_row_block, key_blend, precision=exact_precision
    )
    transition = jnp.einsum("hij,hjk->hik", step_map, transition, precision=exact_precision)
    return ((memory_matrix, transition), None)


def to_blocks(tensor):
    shape_now = tensor.shape
    grouped = tensor.reshape((shape_now[0], shape_now[1] // SPAN, SPAN) + shape_now[2:])
    return jnp.moveaxis(grouped, 1, 0)


def from_blocks(tensor):
    moved = jnp.moveaxis(tensor, 0, 1)
    return moved.reshape((moved.shape[0], moved.shape[1] * moved.shape[2]) + moved.shape[3:])


def delta_outputs(query_rows, key_row_block, value_rows, strength, memory_matrix):
    blocks = (
        to_blocks(query_rows),
        to_blocks(key_row_block),
        to_blocks(value_rows),
        to_blocks(strength),
    )
    memory_end, outputs = lax.scan(span_output, memory_matrix, blocks)
    return (from_blocks(outputs), memory_end)


def apply_map(matrix, tensor):
    return jnp.einsum("hij,hjk->hik", matrix, tensor, precision=exact_precision)


def split_heads(tensor):
    return jnp.transpose(tensor.reshape(tensor.shape[0], H, HD), (1, 0, 2))


def join_heads(tensor):
    return jnp.transpose(tensor, (1, 0, 2)).reshape(tensor.shape[1], H * HD)


def local(
    inputs,
    lengths,
    cotangent,
    norm_gain1,
    w_qkv,
    w_beta,
    conv_weight,
    head_gain,
    w_out,
    norm_gain2,
    w_gateup,
    w_down,
):
    tokens_in = inputs[0].astype(jnp.float32)
    piece_len, model_width = tokens_in.shape
    positions = lax.axis_index("ctx") * piece_len + jnp.arange(piece_len, dtype=jnp.int32)
    valid = (positions < lengths[0]).astype(jnp.float32)
    qkv_full, beta_full, out_full = (
        lax.all_gather(w_qkv, "fsdp", axis=0, tiled=True),
        lax.all_gather(w_beta, "fsdp", axis=0, tiled=True),
        lax.all_gather(w_out, "fsdp", axis=0, tiled=True),
    )
    gateup_full, down_full = (
        lax.all_gather(w_gateup, "fsdp", axis=0, tiled=True),
        lax.all_gather(w_down, "fsdp", axis=0, tiled=True),
    )
    scale_one = lax.rsqrt(jnp.mean(tokens_in * tokens_in, -1, keepdims=True) + 1e-06)
    normed_one = (tokens_in * scale_one * norm_gain1).astype(jnp.bfloat16)
    projected = jnp.dot(normed_one, qkv_full, preferred_element_type=jnp.float32)
    beta_logits = jnp.dot(normed_one, beta_full, preferred_element_type=jnp.float32)
    conv_in = projected * valid[:, None]
    carried_rows = passed_along(
        conv_in[piece_len - KERNEL + 1 :].astype(jnp.bfloat16), "ctx", 1
    ).astype(jnp.float32)
    extended = jnp.concatenate([carried_rows, conv_in], 0)
    conv_pre = conv_weight[0] * extended[0:piece_len]
    for offset in range(1, KERNEL):
        conv_pre = conv_pre + conv_weight[offset] * extended[offset : offset + piece_len]
    gate_conv = jax.nn.sigmoid(conv_pre)
    activated = conv_pre * gate_conv
    raw_queries = split_heads(activated[:, :model_width])
    raw_keys = split_heads(activated[:, model_width : 2 * model_width])
    value_rows = split_heads(activated[:, 2 * model_width :])
    query_scale = lax.rsqrt(jnp.sum(raw_queries * raw_queries, -1, keepdims=True) + 1e-06)
    key_scale = lax.rsqrt(jnp.sum(raw_keys * raw_keys, -1, keepdims=True) + 1e-06)
    query_rows = raw_queries * query_scale * HD ** (-0.5)
    key_row_block = raw_keys * key_scale
    beta_gate = jax.nn.sigmoid(beta_logits)
    strength = jnp.transpose(beta_gate * valid[:, None])
    zero_memory = jnp.zeros((H, HD, HD), jnp.float32)
    identity = jnp.broadcast_to(jnp.eye(HD, dtype=jnp.float32), (H, HD, HD))
    advanced, _ = lax.scan(
        span_advance,
        (zero_memory, identity),
        (to_blocks(key_row_block), to_blocks(value_rows), to_blocks(strength)),
    )
    local_end, transition = advanced

    def relay_forward(step_index, memory_matrix):
        return passed_along(
            (apply_map(transition, memory_matrix) + local_end).astype(jnp.bfloat16), "ctx", 1
        ).astype(jnp.float32)

    memory_in = lax.fori_loop(0, lax.axis_size("ctx") - 1, relay_forward, zero_memory)
    (heads_out, memory_out), pull_back = jax.vjp(
        delta_outputs, query_rows, key_row_block, value_rows, strength, memory_in
    )
    head_scale = lax.rsqrt(jnp.mean(heads_out * heads_out, -1, keepdims=True) + 1e-05)
    merged = join_heads(heads_out * head_scale * head_gain).astype(jnp.bfloat16)
    attention = jnp.dot(merged, out_full, preferred_element_type=jnp.float32)
    middle = tokens_in + attention
    scale_two = lax.rsqrt(jnp.mean(middle * middle, -1, keepdims=True) + 1e-06)
    normed_two = (middle * scale_two * norm_gain2).astype(jnp.bfloat16)
    gate_up = jnp.dot(normed_two, gateup_full, preferred_element_type=jnp.float32)
    ff_width = gate_up.shape[1] // 2
    gate_part = gate_up[:, :ff_width]
    up_part = gate_up[:, ff_width:]
    gate_sig = jax.nn.sigmoid(gate_part)
    hidden = (gate_part * gate_sig * up_part).astype(jnp.bfloat16)
    feed_out = jnp.dot(hidden, down_full, preferred_element_type=jnp.float32)
    output = (middle + feed_out).astype(jnp.bfloat16)
    qkv_back, beta_back, out_back = (
        lax.all_gather(w_qkv, "fsdp", axis=0, tiled=True),
        lax.all_gather(w_beta, "fsdp", axis=0, tiled=True),
        lax.all_gather(w_out, "fsdp", axis=0, tiled=True),
    )
    gateup_back, down_back = (
        lax.all_gather(w_gateup, "fsdp", axis=0, tiled=True),
        lax.all_gather(w_down, "fsdp", axis=0, tiled=True),
    )
    contract_cols = (((1,), (1,)), ((), ()))
    masked_cotangent = cotangent[0].astype(jnp.float32) * valid[:, None]
    grad_feed = masked_cotangent.astype(jnp.bfloat16)
    grad_hidden = lax.dot_general(
        grad_feed, down_back, contract_cols, preferred_element_type=jnp.float32
    )
    grad_gate = grad_hidden * up_part * gate_sig * (1.0 + gate_part * (1.0 - gate_sig))
    grad_up = grad_hidden * gate_part * gate_sig
    grad_gate_up = jnp.concatenate([grad_gate, grad_up], 1).astype(jnp.bfloat16)
    grad_normed_two = lax.dot_general(
        grad_gate_up, gateup_back, contract_cols, preferred_element_type=jnp.float32
    )
    gain_two_term = jnp.sum(grad_normed_two * middle * scale_two, 0)
    scaled_two = grad_normed_two * norm_gain2
    grad_middle = (
        masked_cotangent
        + scale_two * scaled_two
        - scale_two
        * scale_two
        * scale_two
        * middle
        * jnp.mean(scaled_two * middle, -1, keepdims=True)
    )
    grad_attention = grad_middle.astype(jnp.bfloat16)
    grad_merged = lax.dot_general(
        grad_attention, out_back, contract_cols, preferred_element_type=jnp.float32
    )
    grad_heads = split_heads(grad_merged)
    head_gain_term = jnp.sum(grad_heads * heads_out * head_scale, (0, 1))
    scaled_heads = grad_heads * head_gain
    grad_heads_out = (
        head_scale * scaled_heads
        - head_scale
        * head_scale
        * head_scale
        * heads_out
        * jnp.mean(scaled_heads * heads_out, -1, keepdims=True)
    )
    local_grads = pull_back((grad_heads_out, jnp.zeros_like(memory_out)))
    local_part = local_grads[4]
    transposed = jnp.transpose(transition, (0, 2, 1))

    def relay_backward(step_index, memory_grad):
        return passed_along(
            (apply_map(transposed, memory_grad) + local_part).astype(jnp.bfloat16), "ctx", -1
        ).astype(jnp.float32)

    grad_memory_out = lax.fori_loop(0, lax.axis_size("ctx") - 1, relay_backward, zero_memory)
    grad_queries, grad_keys, grad_values, grad_strength, _ = pull_back(
        (grad_heads_out, grad_memory_out)
    )
    grad_beta_logits = (
        jnp.transpose(grad_strength) * valid[:, None] * beta_gate * (1.0 - beta_gate)
    ).astype(jnp.bfloat16)
    grad_raw_queries = HD ** (-0.5) * (
        query_scale * grad_queries
        - query_scale
        * query_scale
        * query_scale
        * raw_queries
        * jnp.sum(raw_queries * grad_queries, -1, keepdims=True)
    )
    grad_raw_keys = key_scale * grad_keys - key_scale * key_scale * key_scale * raw_keys * jnp.sum(
        raw_keys * grad_keys, -1, keepdims=True
    )
    grad_activated = jnp.concatenate(
        [join_heads(grad_raw_queries), join_heads(grad_raw_keys), join_heads(grad_values)], 1
    )
    grad_conv_pre = grad_activated * gate_conv * (1.0 + conv_pre * (1.0 - gate_conv))
    conv_rows = [
        jnp.sum(grad_conv_pre * extended[offset : offset + piece_len], 0)
        for offset in range(KERNEL)
    ]
    conv_term = jnp.stack(conv_rows, 0)
    grad_extended = jnp.pad(conv_weight[0] * grad_conv_pre, ((0, KERNEL - 1), (0, 0)))
    for offset in range(1, KERNEL):
        grad_extended = grad_extended + jnp.pad(
            conv_weight[offset] * grad_conv_pre, ((offset, KERNEL - 1 - offset), (0, 0))
        )
    returned_rows = passed_along(as_sent(grad_extended[: KERNEL - 1]), "ctx", -1)
    grad_conv_in = grad_extended[KERNEL - 1 :] + jnp.pad(
        returned_rows, ((piece_len - KERNEL + 1, 0), (0, 0))
    )
    grad_projected = (grad_conv_in * valid[:, None]).astype(jnp.bfloat16)
    grad_normed_one = lax.dot_general(
        grad_projected, qkv_back, contract_cols, preferred_element_type=jnp.float32
    )
    grad_normed_one = grad_normed_one + lax.dot_general(
        grad_beta_logits, beta_back, contract_cols, preferred_element_type=jnp.float32
    )
    gain_one_term = jnp.sum(grad_normed_one * tokens_in * scale_one, 0)
    scaled_one = grad_normed_one * norm_gain1
    grad_tokens = (
        grad_middle
        + scale_one * scaled_one
        - scale_one
        * scale_one
        * scale_one
        * tokens_in
        * jnp.mean(scaled_one * tokens_in, -1, keepdims=True)
    )
    contract_rows = (((0,), (0,)), ((), ()))
    parts = [
        lax.dot_general(
            normed_one, grad_projected, contract_rows, preferred_element_type=jnp.float32
        ),
        lax.dot_general(merged, grad_attention, contract_rows, preferred_element_type=jnp.float32),
        lax.dot_general(
            normed_two, grad_gate_up, contract_rows, preferred_element_type=jnp.float32
        ),
        lax.dot_general(
            normed_one, grad_beta_logits, contract_rows, preferred_element_type=jnp.float32
        ),
    ]
    wide_share = lax.psum_scatter(
        jnp.concatenate(parts, 1), ("fsdp", "ctx"), scatter_dimension=0, tiled=True
    )
    down_share = lax.psum_scatter(
        lax.dot_general(hidden, grad_feed, contract_rows, preferred_element_type=jnp.float32),
        ("fsdp", "ctx"),
        scatter_dimension=0,
        tiled=True,
    )
    small_sums = lax.psum(
        (gain_one_term, conv_term, head_gain_term, gain_two_term), ("fsdp", "ctx")
    )
    totals = (
        lax.psum(wide_share.astype(jnp.bfloat16), "dp").astype(jnp.float32),
        lax.psum(down_share.astype(jnp.bfloat16), "dp").astype(jnp.float32),
        lax.psum(small_sums[0].astype(jnp.bfloat16), "dp").astype(jnp.float32),
        lax.psum(small_sums[1].astype(jnp.bfloat16), "dp").astype(jnp.float32),
        lax.psum(small_sums[2].astype(jnp.bfloat16), "dp").astype(jnp.float32),
        lax.psum(small_sums[3].astype(jnp.bfloat16), "dp").astype(jnp.float32),
    )
    wide_total = totals[0]
    qkv_cols = 3 * model_width
    out_end = qkv_cols + model_width
    gateup_end = out_end + gate_up.shape[1]
    return (
        output[None],
        grad_tokens.astype(jnp.bfloat16)[None],
        totals[2],
        wide_total[:, :qkv_cols],
        wide_total[:, gateup_end:],
        totals[3],
        totals[4],
        wide_total[:, qkv_cols:out_end],
        totals[5],
        wide_total[:, out_end:gateup_end],
        totals[1],
    )


def solution(mesh):
    placed = (
        P(("dp", "fsdp"), "ctx", None),
        P(("dp", "fsdp")),
        P(("dp", "fsdp"), "ctx", None),
        P(),
        P("fsdp", None),
        P("fsdp", None),
        P(),
        P(),
        P("fsdp", None),
        P(),
        P("fsdp", None),
        P("fsdp", None),
    )
    return jax.shard_map(
        local,
        mesh=mesh,
        in_specs=placed,
        out_specs=(
            P(("dp", "fsdp"), "ctx", None),
            P(("dp", "fsdp"), "ctx", None),
            P(),
            P(("fsdp", "ctx"), None),
            P(("fsdp", "ctx"), None),
            P(),
            P(),
            P(("fsdp", "ctx"), None),
            P(),
            P(("fsdp", "ctx"), None),
            P(("fsdp", "ctx"), None),
        ),
        check_vma=False,
    )
```

profile of v0, /device:TPU:0, one launch (start us, length us, event | category | flops | bytes accessed | tf_op | source)
XLA Modules:
  0.0 2306.2 jit_solution(14385309891945264913)
XLA Ops:
  11.7 14.9 all_gather.21
  27.2 100.5 %all-gather.5.cloned.1.call-done = bf16[1024,3072]{1,0:T(8,128)(2,1)} async-done(((bf16[256,3072]{1,0:T(8,128)(2,1)}), bf16[1024,3072]{1,0:T(8,128)(2,1)}) %all-gather.5.cloned.1.call-update) | async-done | bytes 6291472 | tf_op jit(solution)/shard_map/all_gather | solution.py:127
  127.7 5.6 convolution_multiply_fusion.1
  138.9 12.9 fusion.151
  159.1 413.5 %while.99 = (s32[]{:T(128)}, f32[8,128,128]{2,1,0:T(8,128)S(1)}, f32[8,128,128]{2,1,0:T(8,128)}, f32[8,8,64,128]{3,2,1,0:T(8,128)S(1)}, f32[8,8,64]{2,1,0:T(8,12...) while((s32[]{:T(128)}, f32[8,128,128]{2,1,0:T(8,128)S(1)}, ...), condition=%wide.region_3.5_spmd.clone, body=%wide.region_2.4_spmd.clone.sunk | while | flops 655380544 | bytes 13583016 | solution.py:160
  162.2 40.7 %custom-call.39 = f32[8,1,64,64]{2,3,1,0:T(8,128)} custom-call(f32[8,1,64,64]{3,2,1,0:T(8,128)} %fusion.417), custom_call_target="InvertDiagBlocksLowerTriangular" | custom-call | tf_op jit(solution)/shard_map/while/body/eval_jaxpr/jit(_solve_triangular)/vmap()/triangular_solve/custom-call.1 | solution.py:33
  213.9 40.7 %custom-call.39 = f32[8,1,64,64]{2,3,1,0:T(8,128)} custom-call(f32[8,1,64,64]{3,2,1,0:T(8,128)} %fusion.417), custom_call_target="InvertDiagBlocksLowerTriangular" | custom-call | tf_op jit(solution)/shard_map/while/body/eval_jaxpr/jit(_solve_triangular)/vmap()/triangular_solve/custom-call.1 | solution.py:33
  265.6 40.7 %custom-call.39 = f32[8,1,64,64]{2,3,1,0:T(8,128)} custom-call(f32[8,1,64,64]{3,2,1,0:T(8,128)} %fusion.417), custom_call_target="InvertDiagBlocksLowerTriangular" | custom-call | tf_op jit(solution)/shard_map/while/body/eval_jaxpr/jit(_solve_triangular)/vmap()/triangular_solve/custom-call.1 | solution.py:33
  317.2 40.7 %custom-call.39 = f32[8,1,64,64]{2,3,1,0:T(8,128)} custom-call(f32[8,1,64,64]{3,2,1,0:T(8,128)} %fusion.417), custom_call_target="InvertDiagBlocksLowerTriangular" | custom-call | tf_op jit(solution)/shard_map/while/body/eval_jaxpr/jit(_solve_triangular)/vmap()/triangular_solve/custom-call.1 | solution.py:33
  368.9 40.7 %custom-call.39 = f32[8,1,64,64]{2,3,1,0:T(8,128)} custom-call(f32[8,1,64,64]{3,2,1,0:T(8,128)} %fusion.417), custom_call_target="InvertDiagBlocksLowerTriangular" | custom-call | tf_op jit(solution)/shard_map/while/body/eval_jaxpr/jit(_solve_triangular)/vmap()/triangular_solve/custom-call.1 | solution.py:33
  420.6 40.7 %custom-call.39 = f32[8,1,64,64]{2,3,1,0:T(8,128)} custom-call(f32[8,1,64,64]{3,2,1,0:T(8,128)} %fusion.417), custom_call_target="InvertDiagBlocksLowerTriangular" | custom-call | tf_op jit(solution)/shard_map/while/body/eval_jaxpr/jit(_solve_triangular)/vmap()/triangular_solve/custom-call.1 | solution.py:33
  472.3 40.7 %custom-call.39 = f32[8,1,64,64]{2,3,1,0:T(8,128)} custom-call(f32[8,1,64,64]{3,2,1,0:T(8,128)} %fusion.417), custom_call_target="InvertDiagBlocksLowerTriangular" | custom-call | tf_op jit(solution)/shard_map/while/body/eval_jaxpr/jit(_solve_triangular)/vmap()/triangular_solve/custom-call.1 | solution.py:33
  524.0 40.7 %custom-call.39 = f32[8,1,64,64]{2,3,1,0:T(8,128)} custom-call(f32[8,1,64,64]{3,2,1,0:T(8,128)} %fusion.417), custom_call_target="InvertDiagBlocksLowerTriangular" | custom-call | tf_op jit(solution)/shard_map/while/body/eval_jaxpr/jit(_solve_triangular)/vmap()/triangular_solve/custom-call.1 | solution.py:33
  583.0 469.8 %while.97 = (s32[]{:T(128)}, f32[8,128,128]{2,1,0:T(8,128)S(1)}, f32[8,8,64,128]{3,2,0,1:T(8,128)}, f32[8,8,64,1]{2,1,3,0:T(8,128)S(1)}, f32[8,8,64,64]{3,2,1,0:...) while((s32[]{:T(128)}, f32[8,128,128]{2,1,0:T(8,128)S(1)}, ...), condition=%wide.region_6.8_spmd.clone, body=%wide.region_5.7_spmd.clone.sunk | while | flops 554618944 | bytes 16134973 | solution.py:92
  590.1 40.7 %custom-call.37 = f32[8,1,64,64]{2,3,1,0:T(8,128)} custom-call(f32[8,1,64,64]{3,2,1,0:T(8,128)} %add_bitcast_fusion.4), custom_call_target="InvertDiagBlocksLowerTriangular" | custom-call | tf_op jit(solution)/shard_map/jvp()/while/body/eval_jaxpr/jit(_solve_triangular)/vmap()/triangular_solve/custom-call.1 | solution.py:33
  648.7 40.7 %custom-call.37 = f32[8,1,64,64]{2,3,1,0:T(8,128)} custom-call(f32[8,1,64,64]{3,2,1,0:T(8,128)} %add_bitcast_fusion.4), custom_call_target="InvertDiagBlocksLowerTriangular" | custom-call | tf_op jit(solution)/shard_map/jvp()/while/body/eval_jaxpr/jit(_solve_triangular)/vmap()/triangular_solve/custom-call.1 | solution.py:33
  707.5 40.7 %custom-call.37 = f32[8,1,64,64]{2,3,1,0:T(8,128)} custom-call(f32[8,1,64,64]{3,2,1,0:T(8,128)} %add_bitcast_fusion.4), custom_call_target="InvertDiagBlocksLowerTriangular" | custom-call | tf_op jit(solution)/shard_map/jvp()/while/body/eval_jaxpr/jit(_solve_triangular)/vmap()/triangular_solve/custom-call.1 | solution.py:33
  766.3 40.7 %custom-call.37 = f32[8,1,64,64]{2,3,1,0:T(8,128)} custom-call(f32[8,1,64,64]{3,2,1,0:T(8,128)} %add_bitcast_fusion.4), custom_call_target="InvertDiagBlocksLowerTriangular" | custom-call | tf_op jit(solution)/shard_map/jvp()/while/body/eval_jaxpr/jit(_solve_triangular)/vmap()/triangular_solve/custom-call.1 | solution.py:33
  825.0 40.7 %custom-call.37 = f32[8,1,64,64]{2,3,1,0:T(8,128)} custom-call(f32[8,1,64,64]{3,2,1,0:T(8,128)} %add_bitcast_fusion.4), custom_call_target="InvertDiagBlocksLowerTriangular" | custom-call | tf_op jit(solution)/shard_map/jvp()/while/body/eval_jaxpr/jit(_solve_triangular)/vmap()/triangular_solve/custom-call.1 | solution.py:33
  883.8 40.7 %custom-call.37 = f32[8,1,64,64]{2,3,1,0:T(8,128)} custom-call(f32[8,1,64,64]{3,2,1,0:T(8,128)} %add_bitcast_fusion.4), custom_call_target="InvertDiagBlocksLowerTriangular" | custom-call | tf_op jit(solution)/shard_map/jvp()/while/body/eval_jaxpr/jit(_solve_triangular)/vmap()/triangular_solve/custom-call.1 | solution.py:33
  942.5 40.7 %custom-call.37 = f32[8,1,64,64]{2,3,1,0:T(8,128)} custom-call(f32[8,1,64,64]{3,2,1,0:T(8,128)} %add_bitcast_fusion.4), custom_call_target="InvertDiagBlocksLowerTriangular" | custom-call | tf_op jit(solution)/shard_map/jvp()/while/body/eval_jaxpr/jit(_solve_triangular)/vmap()/triangular_solve/custom-call.1 | solution.py:33
  1001.2 40.7 %custom-call.37 = f32[8,1,64,64]{2,3,1,0:T(8,128)} custom-call(f32[8,1,64,64]{3,2,1,0:T(8,128)} %add_bitcast_fusion.4), custom_call_target="InvertDiagBlocksLowerTriangular" | custom-call | tf_op jit(solution)/shard_map/jvp()/while/body/eval_jaxpr/jit(_solve_triangular)/vmap()/triangular_solve/custom-call.1 | solution.py:33
  1065.0 12.3 fusion.218
  1077.3 11.9 multiply_convert_fusion.1
  1091.8 11.1 fusion.152
  1102.9 13.4 multiply_reduce_fusion.4
  1126.1 48.7 %while.100 = (s32[]{:T(128)}, f32[8,128,128]{2,1,0:T(8,128)S(1)}, f32[8,8,64,128]{3,2,1,0:T(8,128)}, f32[8,8,64,128]{3,2,1,0:T(8,128)}, f32[8,8,64,128]{3,2,1,0:...) while((s32[]{:T(128)}, f32[8,128,128]{2,1,0:T(8,128)S(1)}, ...), condition=%wide.region_12.14_spmd.clone, body=%wide.region_11.13_spmd.clone.sunk | while | flops 352976896 | bytes 5245579 | solution.py:92
  1177.1 9.6 fusion.204
  1198.8 541.7 %while.98 = (s32[]{:T(128)}, f32[8,128,128]{2,1,0:T(8,128)S(1)}, f32[8,8,64,128]{3,2,0,1:T(8,128)}, f32[8,8,64,128]{3,2,0,1:T(8,128)}, f32[8,8,64,128]{3,2,0,1:T...) while((s32[]{:T(128)}, f32[8,128,128]{2,1,0:T(8,128)S(1)}, ...), condition=%wide.region_16.18_spmd.clone.clone, body=%wide.region_13.17_spmd.clone.clone.sunk | while | flops 1134243328 | bytes 18174760 | solution.py:92
  1216.7 40.7 %custom-call.38 = f32[8,1,64,64]{2,3,1,0:T(8,128)} custom-call(f32[8,1,64,64]{3,2,1,0:T(8,128)} %add_bitcast_fusion.5), custom_call_target="InvertDiagBlocksLowerTriangular" | custom-call | tf_op jit(solution)/shard_map/transpose(jvp())/while/body/eval_jaxpr/jit(_solve_triangular)/vmap()/triangular_solve | solution.py:33
  1284.5 40.7 %custom-call.38 = f32[8,1,64,64]{2,3,1,0:T(8,128)} custom-call(f32[8,1,64,64]{3,2,1,0:T(8,128)} %add_bitcast_fusion.5), custom_call_target="InvertDiagBlocksLowerTriangular" | custom-call | tf_op jit(solution)/shard_map/transpose(jvp())/while/body/eval_jaxpr/jit(_solve_triangular)/vmap()/triangular_solve | solution.py:33
  1352.1 40.7 %custom-call.38 = f32[8,1,64,64]{2,3,1,0:T(8,128)} custom-call(f32[8,1,64,64]{3,2,1,0:T(8,128)} %add_bitcast_fusion.5), custom_call_target="InvertDiagBlocksLowerTriangular" | custom-call | tf_op jit(solution)/shard_map/transpose(jvp())/while/body/eval_jaxpr/jit(_solve_triangular)/vmap()/triangular_solve | solution.py:33
  1419.8 40.7 %custom-call.38 = f32[8,1,64,64]{2,3,1,0:T(8,128)} custom-call(f32[8,1,64,64]{3,2,1,0:T(8,128)} %add_bitcast_fusion.5), custom_call_target="InvertDiagBlocksLowerTriangular" | custom-call | tf_op jit(solution)/shard_map/transpose(jvp())/while/body/eval_jaxpr/jit(_solve_triangular)/vmap()/triangular_solve | solution.py:33
  1487.5 40.7 %custom-call.38 = f32[8,1,64,64]{2,3,1,0:T(8,128)} custom-call(f32[8,1,64,64]{3,2,1,0:T(8,128)} %add_bitcast_fusion.5), custom_call_target="InvertDiagBlocksLowerTriangular" | custom-call | tf_op jit(solution)/shard_map/transpose(jvp())/while/body/eval_jaxpr/jit(_solve_triangular)/vmap()/triangular_solve | solution.py:33
  1555.2 40.7 %custom-call.38 = f32[8,1,64,64]{2,3,1,0:T(8,128)} custom-call(f32[8,1,64,64]{3,2,1,0:T(8,128)} %add_bitcast_fusion.5), custom_call_target="InvertDiagBlocksLowerTriangular" | custom-call | tf_op jit(solution)/shard_map/transpose(jvp())/while/body/eval_jaxpr/jit(_solve_triangular)/vmap()/triangular_solve | solution.py:33
  1622.9 40.7 %custom-call.38 = f32[8,1,64,64]{2,3,1,0:T(8,128)} custom-call(f32[8,1,64,64]{3,2,1,0:T(8,128)} %add_bitcast_fusion.5), custom_call_target="InvertDiagBlocksLowerTriangular" | custom-call | tf_op jit(solution)/shard_map/transpose(jvp())/while/body/eval_jaxpr/jit(_solve_triangular)/vmap()/triangular_solve | solution.py:33
  1690.6 40.7 %custom-call.38 = f32[8,1,64,64]{2,3,1,0:T(8,128)} custom-call(f32[8,1,64,64]{3,2,1,0:T(8,128)} %add_bitcast_fusion.5), custom_call_target="InvertDiagBlocksLowerTriangular" | custom-call | tf_op jit(solution)/shard_map/transpose(jvp())/while/body/eval_jaxpr/jit(_solve_triangular)/vmap()/triangular_solve | solution.py:33
  1753.5 5.7 multiply_reduce_fusion.3
  1759.3 6.9 broadcast_multiply_fusion.4
  1766.2 8.1 pad_add_fusion.3
  1778.0 6.9 fusion.221
  1784.9 26.0 %pad_maximum_fusion.2 = f32[1024,9736]{1,0:T(8,128)} fusion(f32[1024,8]{1,0:T(8,128)S(1)} %fusion.219, f32[1024,5632]{1,0:T(8,128)} %fusion.152, f32[1024,1024]{1,0:T(8,128)S(1)} %copy-done.10, f32[1024,3072]{1,0:T(8,128)} %fusion.221), kind=kLoop, calls=%fused_computation.201 | loop fusion | flops 29908992 | bytes 79757312 | tf_op jit(solution)/shard_map/concatenate | solution.py:314
  1813.7 385.5 %reduce-scatter.3.cloned.1.call-done = f32[128,9736]{1,0:T(8,128)} async-done(((f32[1024,9736]{1,0:T(8,128)}), f32[128,9736]{1,0:T(8,128)}) %reduce-scatter.3.cloned.1.call-update) | async-done | bytes 4984848 | tf_op jit(solution)/shard_map/reduce_scatter | solution.py:313
  2204.9 8.7 fusion.194
  2214.2 10.1 fusion.162
  2224.3 26.4 %all-reduce.7 = (bf16[1024]{0:T(1024)(128)(2,1)S(1)}, bf16[4,3072]{1,0:T(4,128)(2,1)S(1)}, bf16[128]{0:T(256)(128)(2,1)S(1)}, bf16[1024]{0:T(1024)(128)(2,1)S(1)}) all-reduce(f32[1024]{0:T(1024)S(1)} %get-tuple-element.1318, f32[4,3072]{1,0:T(4,128)S(1)} %pad_maximum_fusion.7, ...), channel_id=1, replica_groups=mesh['dp'=4,'fsdp'=4,'ctx'=2] {'fsdp','ctx'}, use_global_device_ids=true, to_apply=%region_21.23 | all-reduce | flops 14464 | bytes 86784 | tf_op jit(solution)/shard_map/psum | solution.py:322
  2250.7 16.6 all-reduce.8
  2273.0 18.6 all-reduce.12.cloned.1.call-done
  (779 shorter events, 599.0 us)
Async XLA Ops:
  7.2 120.5 %all-gather.5.cloned.1.call-start = ((), (), s32[]{:S(2)}) async-start(), calls=%async_computation.2 | async-start | bytes 7864320 | tf_op jit(solution)/shard_map/all_gather | solution.py:127
  7.9 1052.2 %all-gather.7.cloned.1.call-start = ((), (), s32[]{:S(2)}) async-start(), calls=%async_computation.3 | async-start | bytes 2621440 | tf_op jit(solution)/shard_map/all_gather | solution.py:129
  8.7 18.0 copy-start.55
  8.7 1056.3 %all-gather.9.cloned.1.call-start = ((), (), s32[]{:S(2)}) async-start(), calls=%async_computation.4 | async-start | bytes 14417920 | tf_op jit(solution)/shard_map/all_gather | solution.py:132
  9.4 1067.9 %all-gather.11.cloned.1.call-start = ((), (), s32[]{:S(2)}) async-start(), calls=%async_computation.5 | async-start | bytes 7208960 | tf_op jit(solution)/shard_map/all_gather | solution.py:133
  10.0 1801.3 %reduce-scatter.5.cloned.1.call-start = ((), (), s32[]{:S(2)}) async-start(), calls=%async_computation.7 | async-start | bytes 12976128 | tf_op jit(solution)/shard_map/reduce_scatter | solution.py:316
  11.6 121.7 %copy-start.50 = (f32[512]{0:T(512)}, f32[512]{0:T(512)S(1)}, u32[]{:S(2)}) copy-start(f32[512]{0:T(512)S(1)} %get-tuple-element.1475) | copy-start | bytes 6148
  11.7 127.2 %copy-start.35 = (f32[1,3072]{1,0:T(1,128)}, f32[1,3072]{1,0:T(1,128)S(1)}, u32[]{:S(2)}) copy-start(f32[1,3072]{1,0:T(1,128)S(1)} %get-tuple-element.1466) | copy-start | bytes 36868
  11.7 127.2 %copy-start.37 = (f32[1,3072]{1,0:T(1,128)}, f32[1,3072]{1,0:T(1,128)S(1)}, u32[]{:S(2)}) copy-start(f32[1,3072]{1,0:T(1,128)S(1)} %get-tuple-element.1467) | copy-start | bytes 36868
  11.7 127.2 %copy-start.39 = (f32[1,3072]{1,0:T(1,128)}, f32[1,3072]{1,0:T(1,128)S(1)}, u32[]{:S(2)}) copy-start(f32[1,3072]{1,0:T(1,128)S(1)} %get-tuple-element.1468) | copy-start | bytes 36868
  11.7 127.2 %copy-start.41 = (f32[1,3072]{1,0:T(1,128)}, f32[1,3072]{1,0:T(1,128)S(1)}, u32[]{:S(2)}) copy-start(f32[1,3072]{1,0:T(1,128)S(1)} %get-tuple-element.1469) | copy-start | bytes 36868
  26.6 106.8 %copy-start.44 = (bf16[1024,8]{0,1:T(8,128)(2,1)}, bf16[1024,8]{0,1:T(8,128)(2,1)S(1)}, u32[]{:S(2)}) copy-start(bf16[1024,8]{0,1:T(8,128)(2,1)S(1)} %all_gather.21) | copy-start | bytes 49156
  27.2 106.2 %copy-start.46 = (f32[512,8]{0,1:T(8,128)}, f32[512,8]{0,1:T(8,128)S(1)}, u32[]{:S(2)}) copy-start(f32[512,8]{0,1:T(8,128)S(1)} %fusion.199) | copy-start | bytes 49156
  136.0 2.8 collective-permute-start
  138.8 13.0 copy-start.30
  572.6 6.5 copy-start.4
  574.4 6.9 collective-permute-start.1
  692.0 5.0 copy-start.1
  750.8 5.0 copy-start.1
  1077.3 14.5 copy-start.16
  1102.9 13.4 copy-start.28
  1126.1 48.7 %copy-start.9 = (f32[8,128,128]{2,1,0:T(8,128)S(1)}, f32[8,128,128]{2,1,0:T(8,128)}, u32[]{:S(2)}) copy-start(f32[8,128,128]{2,1,0:T(8,128)} %get-tuple-element.962) | copy-start | bytes 1572868
  1175.8 17.1 collective-permute-start.2
  1186.8 1012.4 %reduce-scatter.3.cloned.1.call-start = ((), (), s32[]{:S(2)}) async-start(), calls=%async_computation.6 | async-start | bytes 45416448 | tf_op jit(solution)/shard_map/reduce_scatter | solution.py:313
  1257.4 5.2 copy-start.12
  1325.2 5.2 copy-start.12
  1392.8 5.2 copy-start.12
  1460.5 5.2 copy-start.12
  1528.2 5.2 copy-start.12
  1595.9 5.2 copy-start.12
  1663.6 5.2 copy-start.12
  1731.3 5.2 copy-start.12
  1746.3 6.1 slice-start.2
  1753.5 5.8 copy-start.36
  1753.5 5.8 copy-start.38
  1753.5 5.8 copy-start.40
  1753.5 5.8 copy-start.42
  1766.2 9.4 copy-start.47
  1766.2 9.5 copy-start.23
  1766.2 9.5 copy-start.51
  1766.2 9.5 copy-start.56
  1774.4 3.7 collective-permute-start.3
  1778.0 6.9 copy-start.10
  1811.0 480.7 %all-reduce.12.cloned.1.call-start = ((), (), s32[]{:S(2)}) async-start(), calls=%async_computation.8 | async-start | bytes 6488064 | tf_op jit(solution)/shard_map/psum | solution.py:326
  2204.9 8.7 copy-start.45
  2214.2 10.1 copy-start.53
  2214.2 55.5 %copy-start.15 = (f32[512,1024]{1,0:T(8,128)S(1)}, f32[512,1024]{1,0:T(8,128)}, u32[]{:S(2)}) copy-start(f32[512,1024]{1,0:T(8,128)} %copy-done.14) | copy-start | bytes 6291460
  2214.2 55.5 %copy-start.49 = (f32[512]{0:T(512)S(1)}, f32[512]{0:T(512)}, u32[]{:S(2)}) copy-start(f32[512]{0:T(512)} %get-tuple-element.1474) | copy-start | bytes 6148
  (66 other events, 195.4 us)
Sparse Core Ops, SparseCore 0:
  9.6 118.0 all-gather.4
  129.3 44.1 all-gather.6
  175.0 200.9 all-gather.8
  377.4 104.9 all-gather.10
  1186.9 118.9 reduce-scatter.4
  1811.1 388.0 reduce-scatter.2
  2203.5 88.1 all-reduce.11
where the time goes:
time: 2320 us; the launch traced here: 2310 us
  other arithmetic  1100 us (47%)
  matrix products  510 us (22%)
  waiting for transfers between devices  509 us (22%)
  local copies, waits for them, and re-layouts  97.5 us (4%)
  blocking collectives  57.9 us (2%)
    another operation x96, other arithmetic, span_factors(): jax.scipy.linalg.solve_triangular(system, right_side, lower=True, unit_di...  999 us
    reduce_scatter x1, waiting for transfers between devices, local(): lax.psum_scatter(jnp.concatenate(parts, 1), ('fsdp', 'ctx'), scatter_dime...  386 us
    all_gather x1, waiting for transfers between devices, local(): lax.all_gather(w_qkv, 'fsdp', axis=0, tiled=True)  101 us
    another operation x32, matrix products, span_factors(): jax.scipy.linalg.solve_triangular(system, right_side, lower=True, unit_di...  68.7 us
    dot_general x32, matrix products, span_output(): jnp.einsum('ist,itn->isn', query_rows, memory_matrix, precision=exact_pre...  68.5 us
    dot_general x32, matrix products, span_output(): jnp.einsum('ist,itn->isn', key_blend, memory_matrix, precision=exact_prec...  59 us
  transfers between devices with their start and end apart: 11, of which 5 were waited for; matrix products, arithmetic and copies ran while one was open for 69% of the time, Pallas kernels for 0%

commit v1 on v0

--- a/solution.py
+++ b/solution.py
@@ -8,6 +8,24 @@
 KERNEL = 4
 SPAN = 64
 exact_precision = lax.Precision.HIGHEST
+
+
+def gather_around(array, axis, dim):
+    ways, here, step = (lax.axis_size(axis), lax.axis_index(axis), array.shape[dim])
+    dims = [n * ways if d == dim else n for d, n in enumerate(array.shape)]
+    full = lax.dynamic_update_slice_in_dim(
+        jnp.zeros(dims, array.dtype), array, here * step, axis=dim
+    )
+    going_up = going_down = array
+    for far in range(1, ways // 2 + 1):
+        going_up = lax.ppermute(going_up, axis, [(d, (d + 1) % ways) for d in range(ways)])
+        full = lax.dynamic_update_slice_in_dim(full, going_up, (here - far) % ways * step, axis=dim)
+        if 2 * far < ways:
+            going_down = lax.ppermute(going_down, axis, [(d, (d - 1) % ways) for d in range(ways)])
+            full = lax.dynamic_update_slice_in_dim(
+                full, going_down, (here + far) % ways * step, axis=dim
+            )
+    return full
 
 
 def passed_along(value, axis, steps):
@@ -124,7 +142,7 @@
     positions = lax.axis_index("ctx") * piece_len + jnp.arange(piece_len, dtype=jnp.int32)
     valid = (positions < lengths[0]).astype(jnp.float32)
     qkv_full, beta_full, out_full = (
-        lax.all_gather(w_qkv, "fsdp", axis=0, tiled=True),
+        gather_around(w_qkv, "fsdp", 0),
         lax.all_gather(w_beta, "fsdp", axis=0, tiled=True),
         lax.all_gather(w_out, "fsdp", axis=0, tiled=True),
     )

time: 2320 us -> 2550 us (1.099)
  waiting for transfers between devices: 509 us -> 623 us
  blocking collectives: 57.9 us -> 160 us
    all_gather x1, blocking collectives: 14.9 us -> 117 us  [local(): lax.all_gather(w_beta, 'fsdp', axis=0, tiled=True)]
    ppermute x0 -> x3, waiting for transfers between devices: none -> 65.4 us  [the longest x2 65.4 us: gather_around(): lax.ppermute(going_up, axis, [(d, (d + 1) % ways) for d in range(ways)])]
    reduce_scatter x1, waiting for transfers between devices: 386 us -> 421 us  [local(): lax.psum_scatter(jnp.concatenate(parts, 1), ('fsdp', 'ctx'), scatter_dime...]
  transfers between devices with their start and end apart: 11 -> 14, of which waited for: 5 -> 6; matrix products, arithmetic and copies ran while one was open for 69% -> 63% of each run, Pallas kernels for 0% -> 0%
where the time goes in v1:
time: 2550 us; the launch traced here: 2540 us
  other arithmetic  1100 us (43%)
  waiting for transfers between devices  623 us (24%)
  matrix products  511 us (20%)
  blocking collectives  160 us (6%)
  local copies, waits for them, and re-layouts  110 us (4%)
    another operation x96, other arithmetic, span_factors(): jax.scipy.linalg.solve_triangular(system, right_side, lower=True, unit_di...  999 us
    reduce_scatter x1, waiting for transfers between devices, local(): lax.psum_scatter(jnp.concatenate(parts, 1), ('fsdp', 'ctx'), scatter_dime...  421 us
    all_gather x1, blocking collectives, local(): lax.all_gather(w_beta, 'fsdp', axis=0, tiled=True)  117 us
    all_gather x1, waiting for transfers between devices, local(): lax.all_gather(w_qkv, 'fsdp', axis=0, tiled=True)  99 us
    another operation x32, matrix products, span_factors(): jax.scipy.linalg.solve_triangular(system, right_side, lower=True, unit_di...  68.7 us
    dot_general x32, matrix products, span_output(): jnp.einsum('ist,itn->isn', query_rows, memory_matrix, precision=exact_pre...  68.5 us
    ppermute x2, waiting for transfers between devices, gather_around(): lax.ppermute(going_up, axis, [(d, (d + 1) % ways) for d in range(ways)])  65.4 us
    dot_general x32, matrix products, span_output(): jnp.einsum('ist,itn->isn', key_blend, memory_matrix, precision=exact_prec...  59.1 us
  transfers between devices with their start and end apart: 14, of which 6 were waited for; matrix products, arithmetic and copies ran while one was open for 63% of the time, Pallas kernels for 0%

profile of v1, /device:TPU:0, one launch (start us, length us, event | category | flops | bytes accessed | tf_op | source)
XLA Modules:
  0.0 2539.1 jit_solution(10155632397167235328)
XLA Ops:
  14.7 117.1 %all_gather.19 = bf16[1024,8]{0,1:T(8,128)(2,1)S(1)} all-gather(bf16[256,8]{0,1:T(8,128)(2,1)S(1)} %copy-done.55), channel_id=1, replica_groups=mesh['dp'=4,'fsdp'=4,'ctx'=2] {'fsdp'}, dimensions={0}, use_global_device_ids=true | all-gather | bytes 20480 | tf_op jit(solution)/shard_map/all_gather | solution.py:146
  145.3 65.4 %collective-permute-done.2 = bf16[256,3072]{1,0:T(8,128)(2,1)} collective-permute-done((bf16[256,3072]{1,0:T(8,128)(2,1)}, bf16[256,3072]{1,0:T(8,128)(2,1)}, u32[]{:S(2)}, u32[]{:S(2)}) %collective-permute-start.2) | collective-permute-done | bytes 1572896 | tf_op jit(solution)/shard_map/ppermute | solution.py:21
  213.4 5.7 convolution_multiply_fusion.1
  223.9 13.0 fusion.151
  244.3 413.5 %while.99 = (s32[]{:T(128)}, f32[8,128,128]{2,1,0:T(8,128)S(1)}, f32[8,128,128]{2,1,0:T(8,128)}, f32[8,8,64,128]{3,2,1,0:T(8,128)S(1)}, f32[8,8,64]{2,1,0:T(8,12...) while((s32[]{:T(128)}, f32[8,128,128]{2,1,0:T(8,128)S(1)}, ...), condition=%wide.region_3.5_spmd.clone, body=%wide.region_2.4_spmd.clone.sunk | while | flops 655380544 | bytes 13583016 | solution.py:178
  247.4 40.7 %custom-call.39 = f32[8,1,64,64]{2,3,1,0:T(8,128)} custom-call(f32[8,1,64,64]{3,2,1,0:T(8,128)} %fusion.417), custom_call_target="InvertDiagBlocksLowerTriangular" | custom-call | tf_op jit(solution)/shard_map/while/body/eval_jaxpr/jit(_solve_triangular)/vmap()/triangular_solve/custom-call.1 | solution.py:51
  299.0 40.7 %custom-call.39 = f32[8,1,64,64]{2,3,1,0:T(8,128)} custom-call(f32[8,1,64,64]{3,2,1,0:T(8,128)} %fusion.417), custom_call_target="InvertDiagBlocksLowerTriangular" | custom-call | tf_op jit(solution)/shard_map/while/body/eval_jaxpr/jit(_solve_triangular)/vmap()/triangular_solve/custom-call.1 | solution.py:51
  350.8 40.7 %custom-call.39 = f32[8,1,64,64]{2,3,1,0:T(8,128)} custom-call(f32[8,1,64,64]{3,2,1,0:T(8,128)} %fusion.417), custom_call_target="InvertDiagBlocksLowerTriangular" | custom-call | tf_op jit(solution)/shard_map/while/body/eval_jaxpr/jit(_solve_triangular)/vmap()/triangular_solve/custom-call.1 | solution.py:51
  402.5 40.7 %custom-call.39 = f32[8,1,64,64]{2,3,1,0:T(8,128)} custom-call(f32[8,1,64,64]{3,2,1,0:T(8,128)} %fusion.417), custom_call_target="InvertDiagBlocksLowerTriangular" | custom-call | tf_op jit(solution)/shard_map/while/body/eval_jaxpr/jit(_solve_triangular)/vmap()/triangular_solve/custom-call.1 | solution.py:51
  454.1 40.7 %custom-call.39 = f32[8,1,64,64]{2,3,1,0:T(8,128)} custom-call(f32[8,1,64,64]{3,2,1,0:T(8,128)} %fusion.417), custom_call_target="InvertDiagBlocksLowerTriangular" | custom-call | tf_op jit(solution)/shard_map/while/body/eval_jaxpr/jit(_solve_triangular)/vmap()/triangular_solve/custom-call.1 | solution.py:51
  505.8 40.7 %custom-call.39 = f32[8,1,64,64]{2,3,1,0:T(8,128)} custom-call(f32[8,1,64,64]{3,2,1,0:T(8,128)} %fusion.417), custom_call_target="InvertDiagBlocksLowerTriangular" | custom-call | tf_op jit(solution)/shard_map/while/body/eval_jaxpr/jit(_solve_triangular)/vmap()/triangular_solve/custom-call.1 | solution.py:51
  557.5 40.7 %custom-call.39 = f32[8,1,64,64]{2,3,1,0:T(8,128)} custom-call(f32[8,1,64,64]{3,2,1,0:T(8,128)} %fusion.417), custom_call_target="InvertDiagBlocksLowerTriangular" | custom-call | tf_op jit(solution)/shard_map/while/body/eval_jaxpr/jit(_solve_triangular)/vmap()/triangular_solve/custom-call.1 | solution.py:51
  609.2 40.7 %custom-call.39 = f32[8,1,64,64]{2,3,1,0:T(8,128)} custom-call(f32[8,1,64,64]{3,2,1,0:T(8,128)} %fusion.417), custom_call_target="InvertDiagBlocksLowerTriangular" | custom-call | tf_op jit(solution)/shard_map/while/body/eval_jaxpr/jit(_solve_triangular)/vmap()/triangular_solve/custom-call.1 | solution.py:51
  668.1 469.9 %while.97 = (s32[]{:T(128)}, f32[8,128,128]{2,1,0:T(8,128)S(1)}, f32[8,8,64,128]{3,2,0,1:T(8,128)}, f32[8,8,64,1]{2,1,3,0:T(8,128)S(1)}, f32[8,8,64,64]{3,2,1,0:...) while((s32[]{:T(128)}, f32[8,128,128]{2,1,0:T(8,128)S(1)}, ...), condition=%wide.region_6.8_spmd.clone, body=%wide.region_5.7_spmd.clone.sunk | while | flops 554618944 | bytes 16134973 | solution.py:110
  675.1 40.7 %custom-call.37 = f32[8,1,64,64]{2,3,1,0:T(8,128)} custom-call(f32[8,1,64,64]{3,2,1,0:T(8,128)} %add_bitcast_fusion.4), custom_call_target="InvertDiagBlocksLowerTriangular" | custom-call | tf_op jit(solution)/shard_map/jvp()/while/body/eval_jaxpr/jit(_solve_triangular)/vmap()/triangular_solve/custom-call.1 | solution.py:51
  733.8 40.7 %custom-call.37 = f32[8,1,64,64]{2,3,1,0:T(8,128)} custom-call(f32[8,1,64,64]{3,2,1,0:T(8,128)} %add_bitcast_fusion.4), custom_call_target="InvertDiagBlocksLowerTriangular" | custom-call | tf_op jit(solution)/shard_map/jvp()/while/body/eval_jaxpr/jit(_solve_triangular)/vmap()/triangular_solve/custom-call.1 | solution.py:51
  792.5 40.7 %custom-call.37 = f32[8,1,64,64]{2,3,1,0:T(8,128)} custom-call(f32[8,1,64,64]{3,2,1,0:T(8,128)} %add_bitcast_fusion.4), custom_call_target="InvertDiagBlocksLowerTriangular" | custom-call | tf_op jit(solution)/shard_map/jvp()/while/body/eval_jaxpr/jit(_solve_triangular)/vmap()/triangular_solve/custom-call.1 | solution.py:51
  851.4 40.7 %custom-call.37 = f32[8,1,64,64]{2,3,1,0:T(8,128)} custom-call(f32[8,1,64,64]{3,2,1,0:T(8,128)} %add_bitcast_fusion.4), custom_call_target="InvertDiagBlocksLowerTriangular" | custom-call | tf_op jit(solution)/shard_map/jvp()/while/body/eval_jaxpr/jit(_solve_triangular)/vmap()/triangular_solve/custom-call.1 | solution.py:51
  910.1 40.7 %custom-call.37 = f32[8,1,64,64]{2,3,1,0:T(8,128)} custom-call(f32[8,1,64,64]{3,2,1,0:T(8,128)} %add_bitcast_fusion.4), custom_call_target="InvertDiagBlocksLowerTriangular" | custom-call | tf_op jit(solution)/shard_map/jvp()/while/body/eval_jaxpr/jit(_solve_triangular)/vmap()/triangular_solve/custom-call.1 | solution.py:51
  968.8 40.7 %custom-call.37 = f32[8,1,64,64]{2,3,1,0:T(8,128)} custom-call(f32[8,1,64,64]{3,2,1,0:T(8,128)} %add_bitcast_fusion.4), custom_call_target="InvertDiagBlocksLowerTriangular" | custom-call | tf_op jit(solution)/shard_map/jvp()/while/body/eval_jaxpr/jit(_solve_triangular)/vmap()/triangular_solve/custom-call.1 | solution.py:51
  1027.5 40.7 %custom-call.37 = f32[8,1,64,64]{2,3,1,0:T(8,128)} custom-call(f32[8,1,64,64]{3,2,1,0:T(8,128)} %add_bitcast_fusion.4), custom_call_target="InvertDiagBlocksLowerTriangular" | custom-call | tf_op jit(solution)/shard_map/jvp()/while/body/eval_jaxpr/jit(_solve_triangular)/vmap()/triangular_solve/custom-call.1 | solution.py:51
  1086.3 40.7 %custom-call.37 = f32[8,1,64,64]{2,3,1,0:T(8,128)} custom-call(f32[8,1,64,64]{3,2,1,0:T(8,128)} %add_bitcast_fusion.4), custom_call_target="InvertDiagBlocksLowerTriangular" | custom-call | tf_op jit(solution)/shard_map/jvp()/while/body/eval_jaxpr/jit(_solve_triangular)/vmap()/triangular_solve/custom-call.1 | solution.py:51
  1150.1 12.2 fusion.218
  1162.3 11.6 multiply_convert_fusion.1
  1176.5 11.1 fusion.152
  1187.6 13.4 multiply_reduce_fusion.4
  1210.8 48.9 %while.100 = (s32[]{:T(128)}, f32[8,128,128]{2,1,0:T(8,128)S(1)}, f32[8,8,64,128]{3,2,1,0:T(8,128)}, f32[8,8,64,128]{3,2,1,0:T(8,128)}, f32[8,8,64,128]{3,2,1,0:...) while((s32[]{:T(128)}, f32[8,128,128]{2,1,0:T(8,128)S(1)}, ...), condition=%wide.region_12.14_spmd.clone, body=%wide.region_11.13_spmd.clone.sunk | while | flops 352976896 | bytes 5245579 | solution.py:110
  1262.0 9.6 fusion.204
  1283.5 541.7 %while.98 = (s32[]{:T(128)}, f32[8,128,128]{2,1,0:T(8,128)S(1)}, f32[8,8,64,128]{3,2,0,1:T(8,128)}, f32[8,8,64,128]{3,2,0,1:T(8,128)}, f32[8,8,64,128]{3,2,0,1:T...) while((s32[]{:T(128)}, f32[8,128,128]{2,1,0:T(8,128)S(1)}, ...), condition=%wide.region_16.18_spmd.clone.clone, body=%wide.region_13.17_spmd.clone.clone.sunk | while | flops 1134243328 | bytes 18174760 | solution.py:110
  1301.4 40.7 %custom-call.38 = f32[8,1,64,64]{2,3,1,0:T(8,128)} custom-call(f32[8,1,64,64]{3,2,1,0:T(8,128)} %add_bitcast_fusion.5), custom_call_target="InvertDiagBlocksLowerTriangular" | custom-call | tf_op jit(solution)/shard_map/transpose(jvp())/while/body/eval_jaxpr/jit(_solve_triangular)/vmap()/triangular_solve | solution.py:51
  1369.1 40.7 %custom-call.38 = f32[8,1,64,64]{2,3,1,0:T(8,128)} custom-call(f32[8,1,64,64]{3,2,1,0:T(8,128)} %add_bitcast_fusion.5), custom_call_target="InvertDiagBlocksLowerTriangular" | custom-call | tf_op jit(solution)/shard_map/transpose(jvp())/while/body/eval_jaxpr/jit(_solve_triangular)/vmap()/triangular_solve | solution.py:51
  1436.8 40.7 %custom-call.38 = f32[8,1,64,64]{2,3,1,0:T(8,128)} custom-call(f32[8,1,64,64]{3,2,1,0:T(8,128)} %add_bitcast_fusion.5), custom_call_target="InvertDiagBlocksLowerTriangular" | custom-call | tf_op jit(solution)/shard_map/transpose(jvp())/while/body/eval_jaxpr/jit(_solve_triangular)/vmap()/triangular_solve | solution.py:51
  1504.5 40.7 %custom-call.38 = f32[8,1,64,64]{2,3,1,0:T(8,128)} custom-call(f32[8,1,64,64]{3,2,1,0:T(8,128)} %add_bitcast_fusion.5), custom_call_target="InvertDiagBlocksLowerTriangular" | custom-call | tf_op jit(solution)/shard_map/transpose(jvp())/while/body/eval_jaxpr/jit(_solve_triangular)/vmap()/triangular_solve | solution.py:51
  1572.2 40.7 %custom-call.38 = f32[8,1,64,64]{2,3,1,0:T(8,128)} custom-call(f32[8,1,64,64]{3,2,1,0:T(8,128)} %add_bitcast_fusion.5), custom_call_target="InvertDiagBlocksLowerTriangular" | custom-call | tf_op jit(solution)/shard_map/transpose(jvp())/while/body/eval_jaxpr/jit(_solve_triangular)/vmap()/triangular_solve | solution.py:51
  1639.8 40.7 %custom-call.38 = f32[8,1,64,64]{2,3,1,0:T(8,128)} custom-call(f32[8,1,64,64]{3,2,1,0:T(8,128)} %add_bitcast_fusion.5), custom_call_target="InvertDiagBlocksLowerTriangular" | custom-call | tf_op jit(solution)/shard_map/transpose(jvp())/while/body/eval_jaxpr/jit(_solve_triangular)/vmap()/triangular_solve | solution.py:51
  1707.5 40.7 %custom-call.38 = f32[8,1,64,64]{2,3,1,0:T(8,128)} custom-call(f32[8,1,64,64]{3,2,1,0:T(8,128)} %add_bitcast_fusion.5), custom_call_target="InvertDiagBlocksLowerTriangular" | custom-call | tf_op jit(solution)/shard_map/transpose(jvp())/while/body/eval_jaxpr/jit(_solve_triangular)/vmap()/triangular_solve | solution.py:51
  1775.2 40.7 %custom-call.38 = f32[8,1,64,64]{2,3,1,0:T(8,128)} custom-call(f32[8,1,64,64]{3,2,1,0:T(8,128)} %add_bitcast_fusion.5), custom_call_target="InvertDiagBlocksLowerTriangular" | custom-call | tf_op jit(solution)/shard_map/transpose(jvp())/while/body/eval_jaxpr/jit(_solve_triangular)/vmap()/triangular_solve | solution.py:51
  1838.3 5.7 multiply_reduce_fusion.3
  1849.5 6.3 pad_add_fusion.3
  1859.6 6.7 fusion.221
  1866.3 26.1 %pad_maximum_fusion.2 = f32[1024,9736]{1,0:T(8,128)} fusion(f32[1024,8]{1,0:T(8,128)S(1)} %fusion.219, f32[1024,5632]{1,0:T(8,128)} %fusion.152, f32[1024,1024]{1,0:T(8,128)S(1)} %copy-done.10, f32[1024,3072]{1,0:T(8,128)} %fusion.221), kind=kLoop, calls=%fused_computation.201 | loop fusion | flops 29908992 | bytes 79757312 | tf_op jit(solution)/shard_map/concatenate | solution.py:332
  1895.7 421.4 %reduce-scatter.3.cloned.1.call-done = f32[128,9736]{1,0:T(8,128)} async-done(((f32[1024,9736]{1,0:T(8,128)}), f32[128,9736]{1,0:T(8,128)}) %reduce-scatter.3.cloned.1.call-update) | async-done | bytes 4984848 | tf_op jit(solution)/shard_map/reduce_scatter | solution.py:331
  2322.8 8.6 fusion.194
  2333.3 99.0 %all-gather.11.cloned.1.call-done = bf16[1024,3072]{1,0:T(8,128)(2,1)} async-done(((bf16[256,3072]{1,0:T(8,128)(2,1)}), bf16[1024,3072]{1,0:T(8,128)(2,1)}) %all-gather.11.cloned.1.call-update) | async-done | bytes 6291472 | tf_op jit(solution)/shard_map/all_gather | solution.py:209
  2432.3 10.4 fusion.162
  2442.7 26.4 %all-reduce.7 = (bf16[1024]{0:T(1024)(128)(2,1)S(1)}, bf16[4,3072]{1,0:T(4,128)(2,1)S(1)}, bf16[128]{0:T(256)(128)(2,1)S(1)}, bf16[1024]{0:T(1024)(128)(2,1)S(1)}) all-reduce(f32[1024]{0:T(1024)S(1)} %get-tuple-element.1318, f32[4,3072]{1,0:T(4,128)S(1)} %pad_maximum_fusion.7, ...), channel_id=1, replica_groups=mesh['dp'=4,'fsdp'=4,'ctx'=2] {'fsdp','ctx'}, use_global_device_ids=true, to_apply=%region_21.23 | all-reduce | flops 14464 | bytes 86784 | tf_op jit(solution)/shard_map/psum | solution.py:340
  2469.1 16.7 all-reduce.8
  2491.3 33.5 %all-reduce.12.cloned.1.call-done = (bf16[128,9736]{1,0:T(8,128)(2,1)}, bf16[352,1024]{1,0:T(8,128)(2,1)}) async-done(((bf16[128,9736]{1,0:T(8,128)(2,1)}, bf16[352,1024]{1,0:T(8,128)(2,1)}), (bf16[128,9736]{1,0:T(8,128)(2,1)}, bf16[352,1024]{1,0:T(8,128)(2,1)})) %all-reduce.12.cloned.1.call-update) | async-done | bytes 3213328 | tf_op jit(solution)/shard_map/psum | solution.py:344
  (792 shorter events, 623.9 us)
Async XLA Ops:
  7.2 1138.1 %all-gather.5.cloned.1.call-start = ((), (), s32[]{:S(2)}) async-start(), calls=%async_computation.2 | async-start | bytes 2621440 | tf_op jit(solution)/shard_map/all_gather | solution.py:147
  7.9 6.7 copy-start.55
  7.9 123.8 %copy-start.22 = (bf16[1,512,1024]{2,1,0:T(8,128)(2,1)S(1)}, bf16[1,512,1024]{2,1,0:T(8,128)(2,1)}, u32[]{:S(2)}) copy-start(bf16[1,512,1024]{2,1,0:T(8,128)(2,1)} %param.22) | copy-start | bytes 3145732
  7.9 124.7 %copy-start.56 = (f32[1024]{0:T(1024)S(1)}, f32[1024]{0:T(1024)}, u32[]{:S(2)}) copy-start(f32[1024]{0:T(1024)} %param.25) | copy-start | bytes 12292
  8.0 1142.1 %all-gather.7.cloned.1.call-start = ((), (), s32[]{:S(2)}) async-start(), calls=%async_computation.3 | async-start | bytes 14417920 | tf_op jit(solution)/shard_map/all_gather | solution.py:150
  8.7 1153.6 %all-gather.9.cloned.1.call-start = ((), (), s32[]{:S(2)}) async-start(), calls=%async_computation.4 | async-start | bytes 7208960 | tf_op jit(solution)/shard_map/all_gather | solution.py:151
  8.8 129.1 %collective-permute-start = (bf16[256,3072]{1,0:T(8,128)(2,1)S(1)}, bf16[256,3072]{1,0:T(8,128)(2,1)}, u32[]{:S(2)}, u32[]{:S(2)}) collective-permute-start(bf16[256,3072]{1,0:T(8,128)(2,1)S(1)} %copy-done.25), channel_id=1, source_target_pairs={{0,2},{2,4},{4,6},{6,0},{1,3},{3,5},{5,7},{7,1},{8,10},{10,12},{12... | collective-permute-start | bytes 4718600 | tf_op jit(solution)/shard_map/ppermute | solution.py:21
  11.8 130.8 %collective-permute-start.1 = (bf16[256,3072]{1,0:T(8,128)(2,1)S(1)}, bf16[256,3072]{1,0:T(8,128)(2,1)}, u32[]{:S(2)}, u32[]{:S(2)}) collective-permute-start(bf16[256,3072]{1,0:T(8,128)(2,1)S(1)} %copy-done.25), channel_id=1, source_target_pairs={{0,6},{2,0},{4,2},{6,4},{1,7},{3,1},{5,3},{7,5},{8,14},{10,8},{12,... | collective-permute-start | bytes 4718600 | tf_op jit(solution)/shard_map/ppermute | solution.py:24
  14.0 1879.4 %reduce-scatter.5.cloned.1.call-start = ((), (), s32[]{:S(2)}) async-start(), calls=%async_computation.7 | async-start | bytes 12976128 | tf_op jit(solution)/shard_map/reduce_scatter | solution.py:334
  132.6 80.8 %copy-start.51 = (f32[512]{0:T(512)}, f32[512]{0:T(512)S(1)}, u32[]{:S(2)}) copy-start(f32[512]{0:T(512)S(1)} %get-tuple-element.1475) | copy-start | bytes 6148
  137.8 72.9 %collective-permute-start.2 = (bf16[256,3072]{1,0:T(8,128)(2,1)}, bf16[256,3072]{1,0:T(8,128)(2,1)}, u32[]{:S(2)}, u32[]{:S(2)}) collective-permute-start(bf16[256,3072]{1,0:T(8,128)(2,1)} %collective-permute-done), channel_id=1, source_target_pairs={{0,2},{2,4},{4,6},{6,0},{1,3},{3,5},{5,7},{7,1},{8,10},{10,12},{12... | collective-permute-start | bytes 4718600 | tf_op jit(solution)/shard_map/ppermute | solution.py:21
  139.9 84.0 %copy-start.36 = (f32[1,3072]{1,0:T(1,128)}, f32[1,3072]{1,0:T(1,128)S(1)}, u32[]{:S(2)}) copy-start(f32[1,3072]{1,0:T(1,128)S(1)} %get-tuple-element.1466) | copy-start | bytes 36868
  139.9 84.0 %copy-start.38 = (f32[1,3072]{1,0:T(1,128)}, f32[1,3072]{1,0:T(1,128)S(1)}, u32[]{:S(2)}) copy-start(f32[1,3072]{1,0:T(1,128)S(1)} %get-tuple-element.1467) | copy-start | bytes 36868
  139.9 84.0 %copy-start.40 = (f32[1,3072]{1,0:T(1,128)}, f32[1,3072]{1,0:T(1,128)S(1)}, u32[]{:S(2)}) copy-start(f32[1,3072]{1,0:T(1,128)S(1)} %get-tuple-element.1468) | copy-start | bytes 36868
  139.9 84.0 %copy-start.42 = (f32[1,3072]{1,0:T(1,128)}, f32[1,3072]{1,0:T(1,128)S(1)}, u32[]{:S(2)}) copy-start(f32[1,3072]{1,0:T(1,128)S(1)} %get-tuple-element.1469) | copy-start | bytes 36868
  221.7 2.1 collective-permute-start.3
  223.8 13.0 copy-start.31
  657.8 6.4 copy-start.4
  659.5 6.7 collective-permute-start.4
  1162.3 14.2 copy-start.16
  1187.6 13.4 copy-start.29
  1210.8 48.9 %copy-start.9 = (f32[8,128,128]{2,1,0:T(8,128)S(1)}, f32[8,128,128]{2,1,0:T(8,128)}, u32[]{:S(2)}) copy-start(f32[8,128,128]{2,1,0:T(8,128)} %get-tuple-element.962) | copy-start | bytes 1572868
  1260.7 16.9 collective-permute-start.5
  1271.7 1045.4 %reduce-scatter.3.cloned.1.call-start = ((), (), s32[]{:S(2)}) async-start(), calls=%async_computation.6 | async-start | bytes 45416448 | tf_op jit(solution)/shard_map/reduce_scatter | solution.py:331
  1342.1 5.2 copy-start.12
  1409.8 5.2 copy-start.12
  1477.5 5.2 copy-start.12
  1545.2 5.2 copy-start.12
  1612.9 5.2 copy-start.12
  1680.5 5.2 copy-start.12
  1748.2 5.2 copy-start.12
  1831.1 6.1 slice-start.2
  1838.2 5.8 copy-start.37
  1838.2 5.8 copy-start.39
  1838.3 5.8 copy-start.41
  1838.3 5.8 copy-start.43
  1849.5 7.6 copy-start.48
  1849.5 7.7 copy-start.23
  1849.5 7.7 copy-start.52
  1849.5 7.7 copy-start.57
  1855.8 3.7 collective-permute-start.6
  1859.6 6.7 copy-start.10
  1892.4 539.9 %all-gather.11.cloned.1.call-start = ((), (), s32[]{:S(2)}) async-start(), calls=%async_computation.5 | async-start | bytes 7864320 | tf_op jit(solution)/shard_map/all_gather | solution.py:209
  1893.0 631.7 %all-reduce.12.cloned.1.call-start = ((), (), s32[]{:S(2)}) async-start(), calls=%async_computation.8 | async-start | bytes 6488064 | tf_op jit(solution)/shard_map/psum | solution.py:344
  2322.8 8.6 copy-start.46
  2333.3 109.4 %copy-start.54 = (f32[1024]{0:T(1024)S(1)}, f32[1024]{0:T(1024)}, u32[]{:S(2)}) copy-start(f32[1024]{0:T(1024)} %get-tuple-element.1314) | copy-start | bytes 12292
  2333.3 154.8 %copy-start.15 = (f32[512,1024]{1,0:T(8,128)S(1)}, f32[512,1024]{1,0:T(8,128)}, u32[]{:S(2)}) copy-start(f32[512,1024]{1,0:T(8,128)} %copy-done.14) | copy-start | bytes 6291460
  2333.3 154.8 %copy-start.50 = (f32[512]{0:T(512)S(1)}, f32[512]{0:T(512)}, u32[]{:S(2)}) copy-start(f32[512]{0:T(512)} %get-tuple-element.1474) | copy-start | bytes 6148
  (70 other events, 213.3 us)
Sparse Core Ops, SparseCore 0:
  9.6 89.7 all-gather.4
  100.9 234.7 all-gather.6
  337.3 106.1 all-gather.8
  1271.8 155.4 reduce-scatter.4
  1892.5 424.4 reduce-scatter.2
  2318.6 113.7 all-gather.10
  2436.4 88.2 all-reduce.11
